TPU v7x, 256 devices: a whole 4x4x8 slice. The times are simulated.
256 devices in a mesh: sub: 32 (over y_lo, z, core), crow: 4 (over x), ccol: 2 (over y_hi).
Axes of the slice: x: 4, y: 4 (y_hi: 2, y_lo: 2; y = y_hi * 2 + y_lo), z: 8, core: 2. Of those that a mesh axis runs over, the one named last changes fastest.
Arguments:
- rhs: float32 [192, 48, 3, 10, 256], P('sub', ('crow', 'ccol')), may hold values from -6 to 6
- start: float32 [192, 48, 3, 10, 256], P('sub', ('crow', 'ccol')), may hold values from -1.75 to 1.75
- stiffness: float32 [192, 48, 3, 10], P('sub', ('crow', 'ccol')), may hold values from 0.1 to 1
- sub_inverse: bfloat16 [256, 1920, 1920], P(('sub', 'crow', 'ccol')), may hold values from -0.0625 to 0.0625
- basis: bfloat16 [256, 1920, 128], P(('sub', 'crow', 'ccol')), may hold values from -0.0625 to 0.0625
- coarse_inverse: bfloat16 [32, 512, 16384], P(None, ('crow', 'ccol'), 'sub'), may hold values from -0.09375 to 0.09375
- offsets: int32 [32, 8], P('sub'), may hold values from 0 to 464, as said below
Outputs:
- solution: float32 [192, 48, 3, 10, 256], P('sub', ('crow', 'ccol'))
Inputs may be any that keep to these rules, and one draw needn't show every extreme that they name: In every row g, offsets[g, 0] = 0 and the offsets rise; each count (next offset minus this one, 512 after the last) lies between 48 and 128, and every group has a subdomain with exactly 128.
All inputs are finite; a program needn't handle non-finite values.
Results may differ from a plain program's by a relative error of at most 0.0037.
Values may be sent and summed in bfloat16 or wider, within the bound.
A program may use at most 64 MiB of HBM per device.

v0:
```python
import jax
import jax.numpy as jnp
from jax import lax
from jax.sharding import PartitionSpec as P

ITERS = 2


def extended_2(block, sides, width):
    for axis, dim in sides:
        count = lax.axis_size(axis)
        forward = [(i, i + 1) for i in range(count - 1)]
        backward = [(target, source) for source, target in forward]
        low = lax.ppermute(
            lax.slice_in_dim(block, block.shape[dim] - width, None, axis=dim), axis, forward
        )
        high = lax.ppermute(lax.slice_in_dim(block, 0, width, axis=dim), axis, backward)
        block = jnp.concatenate([low, block, high], axis=dim)
    return block


def neighbours(widened):
    padded_z = jnp.pad(widened, ((0, 0), (0, 0), (0, 0), (1, 1), (0, 0)))
    beside = padded_z[2:, 1:-1, :, 1:-1] + padded_z[:-2, 1:-1, :, 1:-1]
    beside = beside + padded_z[1:-1, 2:, :, 1:-1] + padded_z[1:-1, :-2, :, 1:-1]
    beside = beside + padded_z[1:-1, 1:-1, :, 2:] + padded_z[1:-1, 1:-1, :, :-2]
    return beside


def shards(rhs, start, stiffness, sub_inverse, basis, coarse_inverse, offsets):
    cells_s, cells_q, comps, layers, columns = rhs.shape
    kgroup = coarse_inverse.shape[2]
    share_rows = coarse_inverse.shape[1]
    max_cols = basis.shape[2]
    group_offsets = offsets[0]
    groups = group_offsets.shape[0]
    counts = jnp.concatenate([group_offsets[1:], jnp.full((1,), kgroup, jnp.int32)]) - group_offsets
    member = lax.axis_index(("crow", "ccol"))
    sub_index = lax.axis_index("sub")
    member_ids = jnp.arange(groups, dtype=jnp.int32)
    picked = member_ids == member
    own_offset = jnp.sum(jnp.where(picked, group_offsets, 0))
    own_count = jnp.sum(jnp.where(picked, counts, 0))
    col_ids = jnp.arange(max_cols, dtype=jnp.int32)
    wanted = jnp.where(col_ids < own_count, own_offset + col_ids, -1)
    diagonal = (6.0 + stiffness)[..., None]
    flat_inverse = coarse_inverse.reshape(-1, kgroup)
    local_inverse = sub_inverse[0]
    local_basis = basis[0]
    solution = start
    for sweep in range(ITERS):
        widened = extended_2(solution, (("sub", 0), (("crow", "ccol"), 1)), 1)
        residual = rhs - (diagonal * solution - neighbours(widened))
        extended = extended_2(residual.astype(jnp.bfloat16), (("sub", 0), (("crow", "ccol"), 1)), 1)
        flat_res = extended.reshape(-1, columns)
        projected = lax.dot_general(
            local_basis, flat_res, (((0,), (0,)), ((), ())), preferred_element_type=jnp.float32
        )
        restricted = jnp.where(col_ids[:, None] < own_count, projected, 0.0).astype(jnp.bfloat16)
        place_piece = lax.all_gather(restricted, ("crow", "ccol"), axis=0, tiled=True)
        place_row_ids = jnp.arange(place_piece.shape[0], dtype=jnp.int32)
        owner_ids = place_row_ids // max_cols
        column = place_row_ids % max_cols
        matches = member_ids[:, None] == owner_ids[None, :]
        slot_base = jnp.sum(jnp.where(matches, group_offsets[:, None], 0), axis=0)
        slot_limit = jnp.sum(jnp.where(matches, counts[:, None], 0), axis=0)
        targets = jnp.where(column < slot_limit, slot_base + column, -1)
        place_selector = (jnp.arange(kgroup, dtype=jnp.int32)[:, None] == targets[None, :]).astype(
            jnp.bfloat16
        )
        placed_sum = jnp.dot(place_selector, place_piece, preferred_element_type=jnp.float32)
        coefficients = placed_sum.astype(jnp.bfloat16)
        partial_value = jnp.dot(flat_inverse, coefficients, preferred_element_type=jnp.float32)
        summed = lax.psum(partial_value, "sub")
        own_share = lax.dynamic_slice_in_dim(summed, sub_index * share_rows, share_rows, 0)
        amounts = own_share.astype(jnp.bfloat16)
        piece = lax.all_gather(amounts, ("crow", "ccol"), axis=0, tiled=True)
        row_ids = jnp.arange(piece.shape[0], dtype=jnp.int32)
        slot_ids = row_ids % share_rows * groups + row_ids // share_rows
        selector = (wanted[:, None] == slot_ids[None, :]).astype(jnp.bfloat16)
        chosen = jnp.dot(selector, piece, preferred_element_type=jnp.float32)
        chosen = chosen.astype(jnp.bfloat16)
        fine_part = jnp.dot(local_inverse, flat_res, preferred_element_type=jnp.float32)
        coarse_part = jnp.dot(local_basis, chosen, preferred_element_type=jnp.float32)
        correction = (fine_part + coarse_part).reshape(
            cells_s + 2, cells_q + 2, comps, layers, columns
        )
        solution = solution + correction[1:-1, 1:-1]
    return solution


def solution(mesh):
    return jax.shard_map(
        shards,
        mesh=mesh,
        in_specs=(
            P("sub", ("crow", "ccol"), None, None, None),
            P("sub", ("crow", "ccol"), None, None, None),
            P("sub", ("crow", "ccol"), None, None),
            P(("sub", "crow", "ccol"), None, None),
            P(("sub", "crow", "ccol"), None, None),
            P(None, ("crow", "ccol"), "sub"),
            P("sub", None),
        ),
        out_specs=P("sub", ("crow", "ccol"), None, None, None),
        check_vma=False,
    )
```

profile of v0, /device:TPU:8, one launch (start us, length us, event | category | flops | bytes accessed | tf_op | source)
XLA Modules:
  0.0 569.7 jit_solution(5922498140937865681)
XLA Ops:
  5.1 7.1 %collective-permute-start = (f32[1,6,3,10,256]{4,3,2,1,0:T(8,128)S(1)}, f32[1,6,3,10,256]{4,3,2,1,0:T(8,128)S(1)}, u32[]{:S(2)}, u32[]{:S(2)}) collective-permute-start(f32[1,6,3,10,256]{4,3,2,1,0:T(8,128)S(1)} %get-tuple-element.15), channel_id=1, source_target_pairs={{8,0},{16,8},{24,16},{32,24},{40,32},{48,40},{56,48},{64,56},{72,6... | collective-permute-start | bytes 552968 | tf_op jit(solution)/shard_map/ppermute | solution.py:17
  17.8 6.1 %collective-permute-start.3 = (f32[8,1,3,10,256]{4,3,2,1,0:T(8,128)S(1)}, f32[8,1,3,10,256]{4,3,2,1,0:T(8,128)S(1)}, u32[]{:S(2)}, u32[]{:S(2)}) collective-permute-start(f32[8,1,3,10,256]{4,3,2,1,0:T(8,128)S(1)} %get-tuple-element.11), channel_id=1, source_target_pairs={{0,1},{1,2},{2,3},{3,4},{4,5},{5,6},{6,7},{8,9},{9,10},{10,11},{11... | collective-permute-start | bytes 737288 | tf_op jit(solution)/shard_map/ppermute | solution.py:14
  23.9 5.7 %collective-permute-done.2 = f32[8,1,3,10,256]{4,3,2,1,0:T(8,128)S(1)} collective-permute-done((f32[8,1,3,10,256]{4,3,2,1,0:T(8,128)S(1)}, f32[8,1,3,10,256]{4,3,2,1,0:T(8,128)S(1)}, u32[]{:S(2)}, u32[]{:S(2)}) %collective-permute-start.2) | collective-permute-done | bytes 245792 | tf_op jit(solution)/shard_map/ppermute | solution.py:17
  29.6 7.6 %collective-permute-done.3 = f32[8,1,3,10,256]{4,3,2,1,0:T(8,128)S(1)} collective-permute-done((f32[8,1,3,10,256]{4,3,2,1,0:T(8,128)S(1)}, f32[8,1,3,10,256]{4,3,2,1,0:T(8,128)S(1)}, u32[]{:S(2)}, u32[]{:S(2)}) %collective-permute-start.3) | collective-permute-done | bytes 245792 | tf_op jit(solution)/shard_map/ppermute | solution.py:14
  42.1 7.1 %collective-permute-start.5 = (bf16[1,6,3,10,256]{4,3,2,1,0:T(8,128)(2,1)S(1)}, bf16[1,6,3,10,256]{4,3,2,1,0:T(8,128)(2,1)S(1)}, u32[]{:S(2)}, u32[]{:S(2)}) collective-permute-start(bf16[1,6,3,10,256]{4,3,2,1,0:T(8,128)(2,1)S(1)} %get-tuple-element.24), channel_id=1, source_target_pairs={{8,0},{16,8},{24,16},{32,24},{40,32},{48,40},{56,48},{64,56},{72,6... | collective-permute-start | bytes 276488 | tf_op jit(solution)/shard_map/ppermute | solution.py:17
  52.7 5.1 collective-permute-start.6
  63.5 3.8 collective-permute-done.7
  69.7 3.2 reshape.98
  74.6 31.4 %all_gather.12 = bf16[1024,256]{0,1:T(8,128)(2,1)S(1)} all-gather(bf16[128,256]{0,1:T(8,128)(2,1)S(1)} %fusion.34), channel_id=1, replica_groups=mesh['sub'=32,'crow'=4,'ccol'=2] {'crow','ccol'}, dimensions={0}, use_global_device_ids=true | all-gather | bytes 589824 | tf_op jit(solution)/shard_map/all_gather | solution.py:60
  108.9 128.1 %all-reduce.4 = bf16[2048,256]{1,0:T(8,128)(2,1)} all-reduce(f32[2048,256]{1,0:T(8,128)} %convolution_bitcast_fusion.1), channel_id=1, replica_groups=mesh['sub'=32,'crow'=4,'ccol'=2] {'sub'}, use_global_device_ids=true, to_apply=%region_4.5 | all-reduce | flops 524288 | bytes 3145728 | tf_op jit(solution)/shard_map/psum | solution.py:74
  237.8 34.5 %all_gather.13 = bf16[512,256]{1,0:T(8,128)(2,1)S(1)} all-gather(bf16[64,256]{1,0:T(8,128)(2,1)S(1)} %dynamic-slice_convert_fusion.1), channel_id=1, replica_groups=mesh['sub'=32,'crow'=4,'ccol'=2] {'crow','ccol'}, dimensions={0}, use_global_device_ids=true | all-gather | bytes 294912 | tf_op jit(solution)/shard_map/all_gather | solution.py:77
  274.3 7.6 %fusion.8 = f32[1920,256]{0,1:T(8,128)} fusion(f32[256,1920]{1,0:T(8,128)} %fusion.35, bf16[1920,256]{1,0:T(8,128)(2,1)} %reshape.98, bf16[1,1920,1920]{2,1,0:T(8,128)(2,1)} %param.10), kind=kOutput, calls=%fused_computation.16 | convolution fusion | flops 1887928320 | bytes 12288000 | tf_op jit(solution)/shard_map/dot_general | solution.py:83
  284.8 3.4 reshape.100
  297.7 7.5 %collective-permute-done.9 = f32[1,6,3,10,256]{4,3,2,1,0:T(8,128)S(1)} collective-permute-done((f32[1,6,3,10,256]{4,3,2,1,0:T(8,128)S(1)}, f32[1,6,3,10,256]{4,3,2,1,0:T(8,128)S(1)}, u32[]{:S(2)}, u32[]{:S(2)}) %collective-permute-start.9) | collective-permute-done | bytes 184352 | tf_op jit(solution)/shard_map/ppermute | solution.py:14
  306.5 6.2 %collective-permute-start.11 = (f32[8,1,3,10,256]{4,3,2,1,0:T(8,128)S(1)}, f32[8,1,3,10,256]{4,3,2,1,0:T(8,128)S(1)}, u32[]{:S(2)}, u32[]{:S(2)}) collective-permute-start(f32[8,1,3,10,256]{4,3,2,1,0:T(8,128)S(1)} %get-tuple-element.9), channel_id=1, source_target_pairs={{0,1},{1,2},{2,3},{3,4},{4,5},{5,6},{6,7},{8,9},{9,10},{10,11},{11... | collective-permute-start | bytes 737288 | tf_op jit(solution)/shard_map/ppermute | solution.py:14
  312.7 3.6 collective-permute-done.10
  322.7 5.8 %collective-permute-start.13 = (bf16[1,6,3,10,256]{4,3,2,1,0:T(8,128)(2,1)S(1)}, bf16[1,6,3,10,256]{4,3,2,1,0:T(8,128)(2,1)S(1)}, u32[]{:S(2)}, u32[]{:S(2)}) collective-permute-start(bf16[1,6,3,10,256]{4,3,2,1,0:T(8,128)(2,1)S(1)} %get-tuple-element.22), channel_id=1, source_target_pairs={{8,0},{16,8},{24,16},{32,24},{40,32},{48,40},{56,48},{64,56},{72,6... | collective-permute-start | bytes 276488 | tf_op jit(solution)/shard_map/ppermute | solution.py:17
  331.1 5.9 %collective-permute-start.14 = (bf16[8,1,3,10,256]{4,3,2,1,0:T(8,128)(2,1)S(1)}, bf16[8,1,3,10,256]{4,3,2,1,0:T(8,128)(2,1)S(1)}, u32[]{:S(2)}, u32[]{:S(2)}) collective-permute-start(bf16[8,1,3,10,256]{4,3,2,1,0:T(8,128)(2,1)S(1)} %get-tuple-element.17), channel_id=1, source_target_pairs={{0,1},{1,2},{2,3},{3,4},{4,5},{5,6},{6,7},{8,9},{9,10},{10,11},{11... | collective-permute-start | bytes 368648 | tf_op jit(solution)/shard_map/ppermute | solution.py:14
  341.0 5.1 collective-permute-done.15
  352.4 31.3 %all_gather.14 = bf16[1024,256]{0,1:T(8,128)(2,1)S(1)} all-gather(bf16[128,256]{0,1:T(8,128)(2,1)S(1)} %fusion.33), channel_id=1, replica_groups=mesh['sub'=32,'crow'=4,'ccol'=2] {'crow','ccol'}, dimensions={0}, use_global_device_ids=true | all-gather | bytes 589824 | tf_op jit(solution)/shard_map/all_gather | solution.py:60
  386.7 127.4 %all-reduce.5 = bf16[2048,256]{1,0:T(8,128)(2,1)} all-reduce(f32[2048,256]{1,0:T(8,128)} %convolution_bitcast_fusion), channel_id=1, replica_groups=mesh['sub'=32,'crow'=4,'ccol'=2] {'sub'}, use_global_device_ids=true, to_apply=%region_5.6 | all-reduce | flops 524288 | bytes 3145728 | tf_op jit(solution)/shard_map/psum | solution.py:74
  514.9 34.5 %all_gather.15 = bf16[512,256]{1,0:T(8,128)(2,1)S(1)} all-gather(bf16[64,256]{1,0:T(8,128)(2,1)S(1)} %dynamic-slice_convert_fusion), channel_id=1, replica_groups=mesh['sub'=32,'crow'=4,'ccol'=2] {'crow','ccol'}, dimensions={0}, use_global_device_ids=true | all-gather | bytes 294912 | tf_op jit(solution)/shard_map/all_gather | solution.py:77
  551.4 7.6 %fusion.14 = f32[1920,256]{0,1:T(8,128)} fusion(f32[256,1920]{1,0:T(8,128)} %fusion.36, bf16[1920,256]{1,0:T(8,128)(2,1)} %reshape.101, bf16[1,1920,1920]{2,1,0:T(8,128)(2,1)} %param.10), kind=kOutput, calls=%fused_computation.18 | convolution fusion | flops 1887928320 | bytes 12288000 | tf_op jit(solution)/shard_map/dot_general | solution.py:83
  561.8 3.4 reshape.102
  (84 shorter events, 80.2 us)
Async XLA Ops:
  0.0 106.0 %copy-start = (bf16[32,64,512]{2,1,0:T(8,128)(2,1)S(1)}, bf16[32,64,512]{2,1,0:T(8,128)(2,1)}, u32[]{:S(2)}) copy-start(bf16[32,64,512]{2,1,0:T(8,128)(2,1)} %param.12) | copy-start | bytes 6291460
  0.0 12.2 %copy-start.11 = (s32[1,8]{1,0:T(1,128)S(1)}, s32[1,8]{1,0:T(1,128)}, u32[]{:S(2)}) copy-start(s32[1,8]{1,0:T(1,128)} %param.13) | copy-start | bytes 100
  3.1 11.5 %collective-permute-start.1 = (f32[1,6,3,10,256]{4,3,2,1,0:T(8,128)S(1)}, f32[1,6,3,10,256]{4,3,2,1,0:T(8,128)S(1)}, u32[]{:S(2)}, u32[]{:S(2)}) collective-permute-start(f32[1,6,3,10,256]{4,3,2,1,0:T(8,128)S(1)} %get-tuple-element.16), channel_id=1, source_target_pairs={{0,8},{8,16},{16,24},{24,32},{32,40},{40,48},{48,56},{56,64},{64,7... | collective-permute-start | bytes 552968 | tf_op jit(solution)/shard_map/ppermute | solution.py:14
  5.1 11.3 %collective-permute-start = (f32[1,6,3,10,256]{4,3,2,1,0:T(8,128)S(1)}, f32[1,6,3,10,256]{4,3,2,1,0:T(8,128)S(1)}, u32[]{:S(2)}, u32[]{:S(2)}) collective-permute-start(f32[1,6,3,10,256]{4,3,2,1,0:T(8,128)S(1)} %get-tuple-element.15), channel_id=1, source_target_pairs={{8,0},{16,8},{24,16},{32,24},{40,32},{48,40},{56,48},{64,56},{72,6... | collective-permute-start | bytes 552968 | tf_op jit(solution)/shard_map/ppermute | solution.py:17
  16.4 20.9 %copy-start.7 = (f32[1,6,3,10,256]{4,3,2,1,0:T(8,128)}, f32[1,6,3,10,256]{4,3,2,1,0:T(8,128)S(1)}, u32[]{:S(2)}) copy-start(f32[1,6,3,10,256]{4,3,2,1,0:T(8,128)S(1)} %collective-permute-done) | copy-start | bytes 552964
  16.5 13.2 %collective-permute-start.2 = (f32[8,1,3,10,256]{4,3,2,1,0:T(8,128)S(1)}, f32[8,1,3,10,256]{4,3,2,1,0:T(8,128)S(1)}, u32[]{:S(2)}, u32[]{:S(2)}) collective-permute-start(f32[8,1,3,10,256]{4,3,2,1,0:T(8,128)S(1)} %get-tuple-element.12), channel_id=1, source_target_pairs={{1,0},{2,1},{3,2},{4,3},{5,4},{6,5},{7,6},{9,8},{10,9},{11,10},{12... | collective-permute-start | bytes 737288 | tf_op jit(solution)/shard_map/ppermute | solution.py:17
  17.8 19.5 %collective-permute-start.3 = (f32[8,1,3,10,256]{4,3,2,1,0:T(8,128)S(1)}, f32[8,1,3,10,256]{4,3,2,1,0:T(8,128)S(1)}, u32[]{:S(2)}, u32[]{:S(2)}) collective-permute-start(f32[8,1,3,10,256]{4,3,2,1,0:T(8,128)S(1)} %get-tuple-element.11), channel_id=1, source_target_pairs={{0,1},{1,2},{2,3},{3,4},{4,5},{5,6},{6,7},{8,9},{9,10},{10,11},{11... | collective-permute-start | bytes 737288 | tf_op jit(solution)/shard_map/ppermute | solution.py:14
  23.9 14.0 %copy-start.3 = (f32[6,6,3,10,256]{4,3,2,1,0:T(8,128)S(1)}, f32[6,6,3,10,256]{4,3,2,1,0:T(8,128)}, u32[]{:S(2)}) copy-start(f32[6,6,3,10,256]{4,3,2,1,0:T(8,128)} %copy-done.2) | copy-start | bytes 3317764
  23.9 14.0 %copy-start.5 = (f32[6,6,3,10,256]{4,2,3,1,0:T(4,128)S(1)}, f32[6,6,3,10,256]{4,2,3,1,0:T(4,128)}, u32[]{:S(2)}) copy-start(f32[6,6,3,10,256]{4,2,3,1,0:T(4,128)} %param.7) | copy-start | bytes 3317764
  40.2 10.2 %collective-permute-start.4 = (bf16[1,6,3,10,256]{4,3,2,1,0:T(8,128)(2,1)S(1)}, bf16[1,6,3,10,256]{4,3,2,1,0:T(8,128)(2,1)S(1)}, u32[]{:S(2)}, u32[]{:S(2)}) collective-permute-start(bf16[1,6,3,10,256]{4,3,2,1,0:T(8,128)(2,1)S(1)} %get-tuple-element.23), channel_id=1, source_target_pairs={{0,8},{8,16},{16,24},{24,32},{32,40},{40,48},{48,56},{56,64},{64,7... | collective-permute-start | bytes 276488 | tf_op jit(solution)/shard_map/ppermute | solution.py:14
  42.1 9.8 %collective-permute-start.5 = (bf16[1,6,3,10,256]{4,3,2,1,0:T(8,128)(2,1)S(1)}, bf16[1,6,3,10,256]{4,3,2,1,0:T(8,128)(2,1)S(1)}, u32[]{:S(2)}, u32[]{:S(2)}) collective-permute-start(bf16[1,6,3,10,256]{4,3,2,1,0:T(8,128)(2,1)S(1)} %get-tuple-element.24), channel_id=1, source_target_pairs={{8,0},{16,8},{24,16},{32,24},{40,32},{48,40},{56,48},{64,56},{72,6... | collective-permute-start | bytes 276488 | tf_op jit(solution)/shard_map/ppermute | solution.py:17
  52.7 10.8 %collective-permute-start.6 = (bf16[8,1,3,10,256]{4,3,2,1,0:T(8,128)(2,1)}, bf16[8,1,3,10,256]{4,3,2,1,0:T(8,128)(2,1)S(1)}, u32[]{:S(2)}, u32[]{:S(2)}) collective-permute-start(bf16[8,1,3,10,256]{4,3,2,1,0:T(8,128)(2,1)} %get-tuple-element.19), channel_id=1, source_target_pairs={{0,1},{1,2},{2,3},{3,4},{4,5},{5,6},{6,7},{8,9},{9,10},{10,11},{11... | collective-permute-start | bytes 368648 | tf_op jit(solution)/shard_map/ppermute | solution.py:14
  57.9 9.4 %collective-permute-start.7 = (bf16[8,1,3,10,256]{4,3,2,1,0:T(8,128)(2,1)}, bf16[8,1,3,10,256]{4,3,2,1,0:T(8,128)(2,1)}, u32[]{:S(2)}, u32[]{:S(2)}) collective-permute-start(bf16[8,1,3,10,256]{4,3,2,1,0:T(8,128)(2,1)} %get-tuple-element.20), channel_id=1, source_target_pairs={{1,0},{2,1},{3,2},{4,3},{5,4},{6,5},{7,6},{9,8},{10,9},{11,10},{12... | collective-permute-start | bytes 368648 | tf_op jit(solution)/shard_map/ppermute | solution.py:17
  108.9 163.4 %copy-start.10 = (s32[128]{0:T(128)S(1)}, s32[128]{0:T(128)}, u32[]{:S(2)}) copy-start(s32[128]{0:T(128)} %add_select_fusion.4) | copy-start | bytes 1540
  290.5 28.8 %copy-start.1 = (f32[6,6,3,10,256]{4,3,2,1,0:T(8,128)}, f32[6,6,3,10,256]{4,3,2,1,0:T(8,128)S(1)}, u32[]{:S(2)}) copy-start(f32[6,6,3,10,256]{4,3,2,1,0:T(8,128)S(1)} %slice_add_fusion.3) | copy-start | bytes 3317764
  290.6 7.1 %collective-permute-start.8 = (f32[1,6,3,10,256]{4,3,2,1,0:T(8,128)S(1)}, f32[1,6,3,10,256]{4,3,2,1,0:T(8,128)S(1)}, u32[]{:S(2)}, u32[]{:S(2)}) collective-permute-start(f32[1,6,3,10,256]{4,3,2,1,0:T(8,128)S(1)} %get-tuple-element.14), channel_id=1, source_target_pairs={{8,0},{16,8},{24,16},{32,24},{40,32},{48,40},{56,48},{64,56},{72,6... | collective-permute-start | bytes 552968 | tf_op jit(solution)/shard_map/ppermute | solution.py:17
  292.5 12.6 %collective-permute-start.9 = (f32[1,6,3,10,256]{4,3,2,1,0:T(8,128)S(1)}, f32[1,6,3,10,256]{4,3,2,1,0:T(8,128)S(1)}, u32[]{:S(2)}, u32[]{:S(2)}) collective-permute-start(f32[1,6,3,10,256]{4,3,2,1,0:T(8,128)S(1)} %get-tuple-element.13), channel_id=1, source_target_pairs={{0,8},{8,16},{16,24},{24,32},{32,40},{40,48},{48,56},{56,64},{64,7... | collective-permute-start | bytes 552968 | tf_op jit(solution)/shard_map/ppermute | solution.py:14
  305.2 11.2 %collective-permute-start.10 = (f32[8,1,3,10,256]{4,3,2,1,0:T(8,128)S(1)}, f32[8,1,3,10,256]{4,3,2,1,0:T(8,128)S(1)}, u32[]{:S(2)}, u32[]{:S(2)}) collective-permute-start(f32[8,1,3,10,256]{4,3,2,1,0:T(8,128)S(1)} %get-tuple-element.10), channel_id=1, source_target_pairs={{1,0},{2,1},{3,2},{4,3},{5,4},{6,5},{7,6},{9,8},{10,9},{11,10},{12... | collective-permute-start | bytes 737288 | tf_op jit(solution)/shard_map/ppermute | solution.py:17
  306.5 12.9 %copy-start.6 = (f32[6,6,3,10,256]{4,2,3,1,0:T(4,128)S(1)}, f32[6,6,3,10,256]{4,2,3,1,0:T(4,128)}, u32[]{:S(2)}) copy-start(f32[6,6,3,10,256]{4,2,3,1,0:T(4,128)} %param.7) | copy-start | bytes 3317764
  306.5 12.1 %collective-permute-start.11 = (f32[8,1,3,10,256]{4,3,2,1,0:T(8,128)S(1)}, f32[8,1,3,10,256]{4,3,2,1,0:T(8,128)S(1)}, u32[]{:S(2)}, u32[]{:S(2)}) collective-permute-start(f32[8,1,3,10,256]{4,3,2,1,0:T(8,128)S(1)} %get-tuple-element.9), channel_id=1, source_target_pairs={{0,1},{1,2},{2,3},{3,4},{4,5},{5,6},{6,7},{8,9},{9,10},{10,11},{11... | collective-permute-start | bytes 737288 | tf_op jit(solution)/shard_map/ppermute | solution.py:14
  320.7 8.6 %collective-permute-start.12 = (bf16[1,6,3,10,256]{4,3,2,1,0:T(8,128)(2,1)S(1)}, bf16[1,6,3,10,256]{4,3,2,1,0:T(8,128)(2,1)S(1)}, u32[]{:S(2)}, u32[]{:S(2)}) collective-permute-start(bf16[1,6,3,10,256]{4,3,2,1,0:T(8,128)(2,1)S(1)} %get-tuple-element.21), channel_id=1, source_target_pairs={{0,8},{8,16},{16,24},{24,32},{32,40},{40,48},{48,56},{56,64},{64,7... | collective-permute-start | bytes 276488 | tf_op jit(solution)/shard_map/ppermute | solution.py:14
  322.7 8.4 %collective-permute-start.13 = (bf16[1,6,3,10,256]{4,3,2,1,0:T(8,128)(2,1)S(1)}, bf16[1,6,3,10,256]{4,3,2,1,0:T(8,128)(2,1)S(1)}, u32[]{:S(2)}, u32[]{:S(2)}) collective-permute-start(bf16[1,6,3,10,256]{4,3,2,1,0:T(8,128)(2,1)S(1)} %get-tuple-element.22), channel_id=1, source_target_pairs={{8,0},{16,8},{24,16},{32,24},{40,32},{48,40},{56,48},{64,56},{72,6... | collective-permute-start | bytes 276488 | tf_op jit(solution)/shard_map/ppermute | solution.py:17
  331.1 9.8 %collective-permute-start.14 = (bf16[8,1,3,10,256]{4,3,2,1,0:T(8,128)(2,1)S(1)}, bf16[8,1,3,10,256]{4,3,2,1,0:T(8,128)(2,1)S(1)}, u32[]{:S(2)}, u32[]{:S(2)}) collective-permute-start(bf16[8,1,3,10,256]{4,3,2,1,0:T(8,128)(2,1)S(1)} %get-tuple-element.17), channel_id=1, source_target_pairs={{0,1},{1,2},{2,3},{3,4},{4,5},{5,6},{6,7},{8,9},{9,10},{10,11},{11... | collective-permute-start | bytes 368648 | tf_op jit(solution)/shard_map/ppermute | solution.py:14
  337.0 9.1 %collective-permute-start.15 = (bf16[8,1,3,10,256]{4,3,2,1,0:T(8,128)(2,1)S(1)}, bf16[8,1,3,10,256]{4,3,2,1,0:T(8,128)(2,1)S(1)}, u32[]{:S(2)}, u32[]{:S(2)}) collective-permute-start(bf16[8,1,3,10,256]{4,3,2,1,0:T(8,128)(2,1)S(1)} %get-tuple-element.18), channel_id=1, source_target_pairs={{1,0},{2,1},{3,2},{4,3},{5,4},{6,5},{7,6},{9,8},{10,9},{11,10},{12... | collective-permute-start | bytes 368648 | tf_op jit(solution)/shard_map/ppermute | solution.py:17
  (4 other events, 15.2 us)
where the time goes:
time: 571 us; the launch traced here: 570 us
  blocking collectives  387 us (68%)
  starting transfers between devices  58.5 us (10%)
  waiting for transfers between devices  49.3 us (9%)
  matrix products  28.4 us (5%)
  local copies, waits for them, and re-layouts  27.4 us (5%)
  other arithmetic  18.3 us (3%)
    psum x2, blocking collectives, shards(): summed = lax.psum(partial_value, 'sub')  256 us
    all_gather x2, blocking collectives, shards(): piece = lax.all_gather(amounts, ('crow', 'ccol'), axis=0, tiled=True)  69 us
    all_gather x2, blocking collectives, shards(): lax.all_gather(restricted, ('crow', 'ccol'), axis=0, tiled=True)  62.8 us
    ppermute x8, starting transfers between devices, extended_2(): lax.ppermute(lax.slice_in_dim(block, block.shape[dim] - width, None, axis...  31.5 us
    ppermute x8, starting transfers between devices, extended_2(): lax.ppermute(lax.slice_in_dim(block, 0, width, axis=dim), axis, backward)  27 us
    ppermute x8, waiting for transfers between devices, extended_2(): lax.ppermute(lax.slice_in_dim(block, block.shape[dim] - width, None, axis...  25 us
    ppermute x8, waiting for transfers between devices, extended_2(): lax.ppermute(lax.slice_in_dim(block, 0, width, axis=dim), axis, backward)  24.3 us
    dot_general x2, matrix products, shards(): jnp.dot(local_inverse, flat_res, preferred_element_type=jnp.float32)  15.2 us
  transfers between devices with their start and end apart: 16, of which 14 were waited for; matrix products, arithmetic and copies ran while one was open for 1% of the time, Pallas kernels for 0%

commit v1 on v0

--- a/solution.py
+++ b/solution.py
@@ -1,9 +1,23 @@
+import functools
 import jax
 import jax.numpy as jnp
 from jax import lax
 from jax.sharding import PartitionSpec as P
 
 ITERS = 2
+
+
+def slot_manage(values, device_axis):
+    rack = []
+    for _ in range(lax.axis_size(device_axis)):
+        rack.append(values)
+    current_block = jnp.stack(rack, axis=0)
+    step_out = lax.all_to_all(current_block, device_axis, 0, 0)
+    finding = jnp.concatenate(step_out, axis=0)
+    return finding
+
+
+vector_bind = functools.partial(slot_manage, device_axis=("crow", "ccol"))
 
 
 def extended_2(block, sides, width):
@@ -57,7 +71,7 @@
             local_basis, flat_res, (((0,), (0,)), ((), ())), preferred_element_type=jnp.float32
         )
         restricted = jnp.where(col_ids[:, None] < own_count, projected, 0.0).astype(jnp.bfloat16)
-        place_piece = lax.all_gather(restricted, ("crow", "ccol"), axis=0, tiled=True)
+        place_piece = vector_bind(restricted)
         place_row_ids = jnp.arange(place_piece.shape[0], dtype=jnp.int32)
         owner_ids = place_row_ids // max_cols
         column = place_row_ids % max_cols

time: 571 us -> 546 us (0.956)
  blocking collectives: 387 us -> 345 us
  waiting for transfers between devices: 49.3 us -> 60.4 us
  starting transfers between devices: 58.5 us -> 64.5 us
    all_gather x2 -> x0, blocking collectives: 62.8 us -> none  [shards(): lax.all_gather(restricted, ('crow', 'ccol'), axis=0, tiled=True)]
    all_to_all x0 -> x1, blocking collectives: none -> 15.1 us  [slot_manage(): step_out = lax.all_to_all(current_block, device_axis, 0, 0)]
    all_to_all x0 -> x1, waiting for transfers between devices: none -> 8.3 us  [slot_manage(): step_out = lax.all_to_all(current_block, device_axis, 0, 0)]
    all_to_all x0 -> x1, starting transfers between devices: none -> 6.03 us  [slot_manage(): step_out = lax.all_to_all(current_block, device_axis, 0, 0)]
  transfers between devices with their start and end apart: 16 -> 17, of which waited for: 14 -> 17; matrix products, arithmetic and copies ran while one was open for 1% -> 1% of each run, Pallas kernels for 0% -> 0%
where the time goes in v1:
time: 546 us; the launch traced here: 545 us
  blocking collectives  345 us (63%)
  starting transfers between devices  64.5 us (12%)
  waiting for transfers between devices  60.4 us (11%)
  matrix products  28.3 us (5%)
  local copies, waits for them, and re-layouts  28.2 us (5%)
  other arithmetic  17.4 us (3%)
    psum x2, blocking collectives, shards(): summed = lax.psum(partial_value, 'sub')  261 us
    all_gather x2, blocking collectives, shards(): piece = lax.all_gather(amounts, ('crow', 'ccol'), axis=0, tiled=True)  69.1 us
    ppermute x8, starting transfers between devices, extended_2(): lax.ppermute(lax.slice_in_dim(block, block.shape[dim] - width, None, axis...  31.4 us
    ppermute x8, starting transfers between devices, extended_2(): lax.ppermute(lax.slice_in_dim(block, 0, width, axis=dim), axis, backward)  27 us
    ppermute x8, waiting for transfers between devices, extended_2(): lax.ppermute(lax.slice_in_dim(block, block.shape[dim] - width, None, axis...  26.2 us
    ppermute x8, waiting for transfers between devices, extended_2(): lax.ppermute(lax.slice_in_dim(block, 0, width, axis=dim), axis, backward)  25.9 us
    dot_general x2, matrix products, shards(): jnp.dot(local_inverse, flat_res, preferred_element_type=jnp.float32)  15.2 us
    all_to_all x1, blocking collectives, slot_manage(): step_out = lax.all_to_all(current_block, device_axis, 0, 0)  15.1 us
  transfers between devices with their start and end apart: 17, of which 17 were waited for; matrix products, arithmetic and copies ran while one was open for 1% of the time, Pallas kernels for 0%

profile of v1, /device:TPU:8, one launch (start us, length us, event | category | flops | bytes accessed | tf_op | source)
XLA Modules:
  0.0 544.6 jit_solution(9620116732673233271)
XLA Ops:
  3.8 7.1 %collective-permute-start = (f32[1,6,3,10,256]{4,3,2,1,0:T(8,128)S(1)}, f32[1,6,3,10,256]{4,3,2,1,0:T(8,128)S(1)}, u32[]{:S(2)}, u32[]{:S(2)}) collective-permute-start(f32[1,6,3,10,256]{4,3,2,1,0:T(8,128)S(1)} %get-tuple-element.15), channel_id=1, source_target_pairs={{8,0},{16,8},{24,16},{32,24},{40,32},{48,40},{56,48},{64,56},{72,6... | collective-permute-start | bytes 552968 | tf_op jit(solution)/shard_map/ppermute | solution.py:31
  18.8 6.1 %collective-permute-start.3 = (f32[8,1,3,10,256]{4,3,2,1,0:T(8,128)}, f32[8,1,3,10,256]{4,3,2,1,0:T(8,128)S(1)}, u32[]{:S(2)}, u32[]{:S(2)}) collective-permute-start(f32[8,1,3,10,256]{4,3,2,1,0:T(8,128)} %get-tuple-element.11), channel_id=1, source_target_pairs={{0,1},{1,2},{2,3},{3,4},{4,5},{5,6},{6,7},{8,9},{9,10},{10,11},{11... | collective-permute-start | bytes 737288 | tf_op jit(solution)/shard_map/ppermute | solution.py:28
  25.9 5.0 collective-permute-done.2
  30.9 7.7 %collective-permute-done.3 = f32[8,1,3,10,256]{4,3,2,1,0:T(8,128)S(1)} collective-permute-done((f32[8,1,3,10,256]{4,3,2,1,0:T(8,128)}, f32[8,1,3,10,256]{4,3,2,1,0:T(8,128)S(1)}, u32[]{:S(2)}, u32[]{:S(2)}) %collective-permute-start.3) | collective-permute-done | bytes 245792 | tf_op jit(solution)/shard_map/ppermute | solution.py:28
  44.4 7.1 %collective-permute-start.5 = (bf16[1,6,3,10,256]{4,3,2,1,0:T(8,128)(2,1)S(1)}, bf16[1,6,3,10,256]{4,3,2,1,0:T(8,128)(2,1)S(1)}, u32[]{:S(2)}, u32[]{:S(2)}) collective-permute-start(bf16[1,6,3,10,256]{4,3,2,1,0:T(8,128)(2,1)S(1)} %get-tuple-element.24), channel_id=1, source_target_pairs={{8,0},{16,8},{24,16},{32,24},{40,32},{48,40},{56,48},{64,56},{72,6... | collective-permute-start | bytes 276488 | tf_op jit(solution)/shard_map/ppermute | solution.py:31
  54.2 5.1 collective-permute-start.6
  61.2 3.4 collective-permute-done.6
  64.7 3.7 collective-permute-done.7
  75.7 6.0 %all-to-all-start = ((bf16[8,128,256]{2,1,0:T(8,128)(2,1)}), bf16[8,128,256]{2,1,0:T(8,128)(2,1)S(1)}, u32[]{:S(2)}, u32[]{:S(2)}) async-start(bf16[8,128,256]{2,1,0:T(8,128)(2,1)} %stack.4), calls=%async_computation | async-start | bytes 1048576 | tf_op jit(solution)/shard_map/all_to_all | solution.py:15
  83.1 8.3 %all-to-all-done = bf16[8,128,256]{2,1,0:T(8,128)(2,1)S(1)} async-done(((bf16[8,128,256]{2,1,0:T(8,128)(2,1)}), bf16[8,128,256]{2,1,0:T(8,128)(2,1)S(1)}, u32[]{:S(2)}, u32[]{:S(2)}) %all-to-all-start) | async-done | bytes 524320 | tf_op jit(solution)/shard_map/all_to_all | solution.py:15
  94.3 131.4 %all-reduce.4 = bf16[2048,256]{1,0:T(8,128)(2,1)} all-reduce(f32[2048,256]{1,0:T(8,128)} %convolution_bitcast_fusion.1), channel_id=1, replica_groups=mesh['sub'=32,'crow'=4,'ccol'=2] {'sub'}, use_global_device_ids=true, to_apply=%region_4.5 | all-reduce | flops 524288 | bytes 3145728 | tf_op jit(solution)/shard_map/psum | solution.py:88
  226.4 34.5 %all_gather.6 = bf16[512,256]{1,0:T(8,128)(2,1)S(1)} all-gather(bf16[64,256]{1,0:T(8,128)(2,1)S(1)} %dynamic-slice_convert_fusion.1), channel_id=1, replica_groups=mesh['sub'=32,'crow'=4,'ccol'=2] {'crow','ccol'}, dimensions={0}, use_global_device_ids=true | all-gather | bytes 294912 | tf_op jit(solution)/shard_map/all_gather | solution.py:91
  262.9 7.6 %fusion.8 = f32[1920,256]{0,1:T(8,128)} fusion(f32[256,1920]{1,0:T(8,128)} %fusion.35, bf16[1920,256]{1,0:T(8,128)(2,1)} %reshape.108, bf16[1,1920,1920]{2,1,0:T(8,128)(2,1)} %param.10), kind=kOutput, calls=%fused_computation.16 | convolution fusion | flops 1887928320 | bytes 12288000 | tf_op jit(solution)/shard_map/dot_general | solution.py:97
  273.4 3.4 reshape.111
  286.3 7.3 %collective-permute-done.9 = f32[1,6,3,10,256]{4,3,2,1,0:T(8,128)S(1)} collective-permute-done((f32[1,6,3,10,256]{4,3,2,1,0:T(8,128)S(1)}, f32[1,6,3,10,256]{4,3,2,1,0:T(8,128)S(1)}, u32[]{:S(2)}, u32[]{:S(2)}) %collective-permute-start.9) | collective-permute-done | bytes 184352 | tf_op jit(solution)/shard_map/ppermute | solution.py:28
  295.1 6.2 %collective-permute-start.11 = (f32[8,1,3,10,256]{4,3,2,1,0:T(8,128)S(1)}, f32[8,1,3,10,256]{4,3,2,1,0:T(8,128)S(1)}, u32[]{:S(2)}, u32[]{:S(2)}) collective-permute-start(f32[8,1,3,10,256]{4,3,2,1,0:T(8,128)S(1)} %get-tuple-element.9), channel_id=1, source_target_pairs={{0,1},{1,2},{2,3},{3,4},{4,5},{5,6},{6,7},{8,9},{9,10},{10,11},{11... | collective-permute-start | bytes 737288 | tf_op jit(solution)/shard_map/ppermute | solution.py:28
  301.3 3.6 collective-permute-done.10
  311.2 5.8 %collective-permute-start.13 = (bf16[1,6,3,10,256]{4,3,2,1,0:T(8,128)(2,1)S(1)}, bf16[1,6,3,10,256]{4,3,2,1,0:T(8,128)(2,1)S(1)}, u32[]{:S(2)}, u32[]{:S(2)}) collective-permute-start(bf16[1,6,3,10,256]{4,3,2,1,0:T(8,128)(2,1)S(1)} %get-tuple-element.22), channel_id=1, source_target_pairs={{8,0},{16,8},{24,16},{32,24},{40,32},{48,40},{56,48},{64,56},{72,6... | collective-permute-start | bytes 276488 | tf_op jit(solution)/shard_map/ppermute | solution.py:31
  319.7 5.9 %collective-permute-start.14 = (bf16[8,1,3,10,256]{4,3,2,1,0:T(8,128)(2,1)S(1)}, bf16[8,1,3,10,256]{4,3,2,1,0:T(8,128)(2,1)S(1)}, u32[]{:S(2)}, u32[]{:S(2)}) collective-permute-start(bf16[8,1,3,10,256]{4,3,2,1,0:T(8,128)(2,1)S(1)} %get-tuple-element.17), channel_id=1, source_target_pairs={{0,1},{1,2},{2,3},{3,4},{4,5},{5,6},{6,7},{8,9},{9,10},{10,11},{11... | collective-permute-start | bytes 368648 | tf_op jit(solution)/shard_map/ppermute | solution.py:28
  328.9 5.8 %collective-permute-done.15 = bf16[8,1,3,10,256]{4,3,2,1,0:T(8,128)(2,1)S(1)} collective-permute-done((bf16[8,1,3,10,256]{4,3,2,1,0:T(8,128)(2,1)S(1)}, bf16[8,1,3,10,256]{4,3,2,1,0:T(8,128)(2,1)S(1)}, u32[]{:S(2)}, u32[]{:S(2)}) %collective-permute-start.15) | collective-permute-done | bytes 122912 | tf_op jit(solution)/shard_map/ppermute | solution.py:31
  341.2 15.1 %all_to_all.10 = bf16[8,128,256]{2,1,0:T(8,128)(2,1)S(1)} all-to-all(bf16[8,128,256]{2,1,0:T(8,128)(2,1)S(1)} %stack.5), channel_id=1, replica_groups=mesh['sub'=32,'crow'=4,'ccol'=2] {'crow','ccol'}, dimensions={0} | all-to-all | bytes 1048576 | tf_op jit(solution)/shard_map/all_to_all | solution.py:15
  359.2 129.7 %all-reduce.5 = bf16[2048,256]{1,0:T(8,128)(2,1)} all-reduce(f32[2048,256]{1,0:T(8,128)} %convolution_bitcast_fusion), channel_id=1, replica_groups=mesh['sub'=32,'crow'=4,'ccol'=2] {'sub'}, use_global_device_ids=true, to_apply=%region_5.6 | all-reduce | flops 524288 | bytes 3145728 | tf_op jit(solution)/shard_map/psum | solution.py:88
  489.7 34.6 %all_gather.7 = bf16[512,256]{1,0:T(8,128)(2,1)S(1)} all-gather(bf16[64,256]{1,0:T(8,128)(2,1)S(1)} %dynamic-slice_convert_fusion), channel_id=1, replica_groups=mesh['sub'=32,'crow'=4,'ccol'=2] {'crow','ccol'}, dimensions={0}, use_global_device_ids=true | all-gather | bytes 294912 | tf_op jit(solution)/shard_map/all_gather | solution.py:91
  526.3 7.6 %fusion.14 = f32[1920,256]{0,1:T(8,128)} fusion(f32[256,1920]{1,0:T(8,128)} %fusion.36, bf16[1920,256]{1,0:T(8,128)(2,1)} %reshape.112, bf16[1,1920,1920]{2,1,0:T(8,128)(2,1)} %param.10), kind=kOutput, calls=%fused_computation.18 | convolution fusion | flops 1887928320 | bytes 12288000 | tf_op jit(solution)/shard_map/dot_general | solution.py:97
  (87 shorter events, 86.1 us)
Async XLA Ops:
  0.0 91.4 %copy-start = (bf16[32,64,512]{2,1,0:T(8,128)(2,1)S(1)}, bf16[32,64,512]{2,1,0:T(8,128)(2,1)}, u32[]{:S(2)}) copy-start(bf16[32,64,512]{2,1,0:T(8,128)(2,1)} %param.12) | copy-start | bytes 6291460
  0.0 13.4 %copy-start.4 = (f32[6,6,3,10,256]{4,2,3,1,0:T(4,128)S(1)}, f32[6,6,3,10,256]{4,2,3,1,0:T(4,128)}, u32[]{:S(2)}) copy-start(f32[6,6,3,10,256]{4,2,3,1,0:T(4,128)} %param.8) | copy-start | bytes 3317764
  1.9 11.5 %collective-permute-start.1 = (f32[1,6,3,10,256]{4,3,2,1,0:T(8,128)S(1)}, f32[1,6,3,10,256]{4,3,2,1,0:T(8,128)S(1)}, u32[]{:S(2)}, u32[]{:S(2)}) collective-permute-start(f32[1,6,3,10,256]{4,3,2,1,0:T(8,128)S(1)} %get-tuple-element.16), channel_id=1, source_target_pairs={{0,8},{8,16},{16,24},{24,32},{32,40},{40,48},{48,56},{56,64},{64,7... | collective-permute-start | bytes 552968 | tf_op jit(solution)/shard_map/ppermute | solution.py:28
  3.8 11.3 %collective-permute-start = (f32[1,6,3,10,256]{4,3,2,1,0:T(8,128)S(1)}, f32[1,6,3,10,256]{4,3,2,1,0:T(8,128)S(1)}, u32[]{:S(2)}, u32[]{:S(2)}) collective-permute-start(f32[1,6,3,10,256]{4,3,2,1,0:T(8,128)S(1)} %get-tuple-element.15), channel_id=1, source_target_pairs={{8,0},{16,8},{24,16},{32,24},{40,32},{48,40},{56,48},{64,56},{72,6... | collective-permute-start | bytes 552968 | tf_op jit(solution)/shard_map/ppermute | solution.py:31
  17.5 13.4 %collective-permute-start.2 = (f32[8,1,3,10,256]{4,3,2,1,0:T(8,128)}, f32[8,1,3,10,256]{4,3,2,1,0:T(8,128)S(1)}, u32[]{:S(2)}, u32[]{:S(2)}) collective-permute-start(f32[8,1,3,10,256]{4,3,2,1,0:T(8,128)} %get-tuple-element.12), channel_id=1, source_target_pairs={{1,0},{2,1},{3,2},{4,3},{5,4},{6,5},{7,6},{9,8},{10,9},{11,10},{12... | collective-permute-start | bytes 737288 | tf_op jit(solution)/shard_map/ppermute | solution.py:31
  18.8 19.8 %collective-permute-start.3 = (f32[8,1,3,10,256]{4,3,2,1,0:T(8,128)}, f32[8,1,3,10,256]{4,3,2,1,0:T(8,128)S(1)}, u32[]{:S(2)}, u32[]{:S(2)}) collective-permute-start(f32[8,1,3,10,256]{4,3,2,1,0:T(8,128)} %get-tuple-element.11), channel_id=1, source_target_pairs={{0,1},{1,2},{2,3},{3,4},{4,5},{5,6},{6,7},{8,9},{9,10},{10,11},{11... | collective-permute-start | bytes 737288 | tf_op jit(solution)/shard_map/ppermute | solution.py:28
  25.9 15.0 %copy-start.3 = (f32[8,6,3,10,256]{4,3,2,1,0:T(8,128)S(1)}, f32[8,6,3,10,256]{4,3,2,1,0:T(8,128)}, u32[]{:S(2)}) copy-start(f32[8,6,3,10,256]{4,3,2,1,0:T(8,128)} %copy-done.2) | copy-start | bytes 4423684
  25.9 15.0 %copy-start.6 = (f32[6,6,3,10,256]{4,3,2,1,0:T(8,128)S(1)}, f32[6,6,3,10,256]{4,3,2,1,0:T(8,128)}, u32[]{:S(2)}) copy-start(f32[6,6,3,10,256]{4,3,2,1,0:T(8,128)} %copy-done.5) | copy-start | bytes 3317764
  25.9 15.0 %copy-start.8 = (f32[6,6,3,10,256]{4,2,3,1,0:T(4,128)S(1)}, f32[6,6,3,10,256]{4,2,3,1,0:T(4,128)}, u32[]{:S(2)}) copy-start(f32[6,6,3,10,256]{4,2,3,1,0:T(4,128)} %param.7) | copy-start | bytes 3317764
  42.5 9.9 %collective-permute-start.4 = (bf16[1,6,3,10,256]{4,3,2,1,0:T(8,128)(2,1)S(1)}, bf16[1,6,3,10,256]{4,3,2,1,0:T(8,128)(2,1)S(1)}, u32[]{:S(2)}, u32[]{:S(2)}) collective-permute-start(bf16[1,6,3,10,256]{4,3,2,1,0:T(8,128)(2,1)S(1)} %get-tuple-element.23), channel_id=1, source_target_pairs={{0,8},{8,16},{16,24},{24,32},{32,40},{40,48},{48,56},{56,64},{64,7... | collective-permute-start | bytes 276488 | tf_op jit(solution)/shard_map/ppermute | solution.py:28
  44.4 9.7 %collective-permute-start.5 = (bf16[1,6,3,10,256]{4,3,2,1,0:T(8,128)(2,1)S(1)}, bf16[1,6,3,10,256]{4,3,2,1,0:T(8,128)(2,1)S(1)}, u32[]{:S(2)}, u32[]{:S(2)}) collective-permute-start(bf16[1,6,3,10,256]{4,3,2,1,0:T(8,128)(2,1)S(1)} %get-tuple-element.24), channel_id=1, source_target_pairs={{8,0},{16,8},{24,16},{32,24},{40,32},{48,40},{56,48},{64,56},{72,6... | collective-permute-start | bytes 276488 | tf_op jit(solution)/shard_map/ppermute | solution.py:31
  54.2 10.5 %collective-permute-start.6 = (bf16[8,1,3,10,256]{4,3,2,1,0:T(8,128)(2,1)S(1)}, bf16[8,1,3,10,256]{4,3,2,1,0:T(8,128)(2,1)S(1)}, u32[]{:S(2)}, u32[]{:S(2)}) collective-permute-start(bf16[8,1,3,10,256]{4,3,2,1,0:T(8,128)(2,1)S(1)} %get-tuple-element.19), channel_id=1, source_target_pairs={{0,1},{1,2},{2,3},{3,4},{4,5},{5,6},{6,7},{8,9},{9,10},{10,11},{11... | collective-permute-start | bytes 368648 | tf_op jit(solution)/shard_map/ppermute | solution.py:28
  59.3 9.1 %collective-permute-start.7 = (bf16[8,1,3,10,256]{4,3,2,1,0:T(8,128)(2,1)S(1)}, bf16[8,1,3,10,256]{4,3,2,1,0:T(8,128)(2,1)S(1)}, u32[]{:S(2)}, u32[]{:S(2)}) collective-permute-start(bf16[8,1,3,10,256]{4,3,2,1,0:T(8,128)(2,1)S(1)} %get-tuple-element.20), channel_id=1, source_target_pairs={{1,0},{2,1},{3,2},{4,3},{5,4},{6,5},{7,6},{9,8},{10,9},{11,10},{12... | collective-permute-start | bytes 368648 | tf_op jit(solution)/shard_map/ppermute | solution.py:31
  75.7 15.7 %all-to-all-start = ((bf16[8,128,256]{2,1,0:T(8,128)(2,1)}), bf16[8,128,256]{2,1,0:T(8,128)(2,1)S(1)}, u32[]{:S(2)}, u32[]{:S(2)}) async-start(bf16[8,128,256]{2,1,0:T(8,128)(2,1)} %stack.4), calls=%async_computation | async-start | bytes 1048576 | tf_op jit(solution)/shard_map/all_to_all | solution.py:15
  279.1 28.8 %copy-start.1 = (f32[6,6,3,10,256]{4,3,2,1,0:T(8,128)}, f32[6,6,3,10,256]{4,3,2,1,0:T(8,128)S(1)}, u32[]{:S(2)}) copy-start(f32[6,6,3,10,256]{4,3,2,1,0:T(8,128)S(1)} %slice_add_fusion.3) | copy-start | bytes 3317764
  279.2 7.2 %collective-permute-start.8 = (f32[1,6,3,10,256]{4,3,2,1,0:T(8,128)S(1)}, f32[1,6,3,10,256]{4,3,2,1,0:T(8,128)S(1)}, u32[]{:S(2)}, u32[]{:S(2)}) collective-permute-start(f32[1,6,3,10,256]{4,3,2,1,0:T(8,128)S(1)} %get-tuple-element.14), channel_id=1, source_target_pairs={{8,0},{16,8},{24,16},{32,24},{40,32},{48,40},{56,48},{64,56},{72,6... | collective-permute-start | bytes 552968 | tf_op jit(solution)/shard_map/ppermute | solution.py:31
  281.1 12.6 %collective-permute-start.9 = (f32[1,6,3,10,256]{4,3,2,1,0:T(8,128)S(1)}, f32[1,6,3,10,256]{4,3,2,1,0:T(8,128)S(1)}, u32[]{:S(2)}, u32[]{:S(2)}) collective-permute-start(f32[1,6,3,10,256]{4,3,2,1,0:T(8,128)S(1)} %get-tuple-element.13), channel_id=1, source_target_pairs={{0,8},{8,16},{16,24},{24,32},{32,40},{40,48},{48,56},{56,64},{64,7... | collective-permute-start | bytes 552968 | tf_op jit(solution)/shard_map/ppermute | solution.py:28
  293.8 11.2 %collective-permute-start.10 = (f32[8,1,3,10,256]{4,3,2,1,0:T(8,128)S(1)}, f32[8,1,3,10,256]{4,3,2,1,0:T(8,128)S(1)}, u32[]{:S(2)}, u32[]{:S(2)}) collective-permute-start(f32[8,1,3,10,256]{4,3,2,1,0:T(8,128)S(1)} %get-tuple-element.10), channel_id=1, source_target_pairs={{1,0},{2,1},{3,2},{4,3},{5,4},{6,5},{7,6},{9,8},{10,9},{11,10},{12... | collective-permute-start | bytes 737288 | tf_op jit(solution)/shard_map/ppermute | solution.py:31
  295.1 12.9 %copy-start.9 = (f32[6,6,3,10,256]{4,2,3,1,0:T(4,128)S(1)}, f32[6,6,3,10,256]{4,2,3,1,0:T(4,128)}, u32[]{:S(2)}) copy-start(f32[6,6,3,10,256]{4,2,3,1,0:T(4,128)} %param.7) | copy-start | bytes 3317764
  295.1 12.1 %collective-permute-start.11 = (f32[8,1,3,10,256]{4,3,2,1,0:T(8,128)S(1)}, f32[8,1,3,10,256]{4,3,2,1,0:T(8,128)S(1)}, u32[]{:S(2)}, u32[]{:S(2)}) collective-permute-start(f32[8,1,3,10,256]{4,3,2,1,0:T(8,128)S(1)} %get-tuple-element.9), channel_id=1, source_target_pairs={{0,1},{1,2},{2,3},{3,4},{4,5},{5,6},{6,7},{8,9},{9,10},{10,11},{11... | collective-permute-start | bytes 737288 | tf_op jit(solution)/shard_map/ppermute | solution.py:28
  309.3 8.6 %collective-permute-start.12 = (bf16[1,6,3,10,256]{4,3,2,1,0:T(8,128)(2,1)S(1)}, bf16[1,6,3,10,256]{4,3,2,1,0:T(8,128)(2,1)S(1)}, u32[]{:S(2)}, u32[]{:S(2)}) collective-permute-start(bf16[1,6,3,10,256]{4,3,2,1,0:T(8,128)(2,1)S(1)} %get-tuple-element.21), channel_id=1, source_target_pairs={{0,8},{8,16},{16,24},{24,32},{32,40},{40,48},{48,56},{56,64},{64,7... | collective-permute-start | bytes 276488 | tf_op jit(solution)/shard_map/ppermute | solution.py:28
  311.2 8.4 %collective-permute-start.13 = (bf16[1,6,3,10,256]{4,3,2,1,0:T(8,128)(2,1)S(1)}, bf16[1,6,3,10,256]{4,3,2,1,0:T(8,128)(2,1)S(1)}, u32[]{:S(2)}, u32[]{:S(2)}) collective-permute-start(bf16[1,6,3,10,256]{4,3,2,1,0:T(8,128)(2,1)S(1)} %get-tuple-element.22), channel_id=1, source_target_pairs={{8,0},{16,8},{24,16},{32,24},{40,32},{48,40},{56,48},{64,56},{72,6... | collective-permute-start | bytes 276488 | tf_op jit(solution)/shard_map/ppermute | solution.py:31
  319.7 9.2 %collective-permute-start.14 = (bf16[8,1,3,10,256]{4,3,2,1,0:T(8,128)(2,1)S(1)}, bf16[8,1,3,10,256]{4,3,2,1,0:T(8,128)(2,1)S(1)}, u32[]{:S(2)}, u32[]{:S(2)}) collective-permute-start(bf16[8,1,3,10,256]{4,3,2,1,0:T(8,128)(2,1)S(1)} %get-tuple-element.17), channel_id=1, source_target_pairs={{0,1},{1,2},{2,3},{3,4},{4,5},{5,6},{6,7},{8,9},{9,10},{10,11},{11... | collective-permute-start | bytes 368648 | tf_op jit(solution)/shard_map/ppermute | solution.py:28
  325.6 9.1 %collective-permute-start.15 = (bf16[8,1,3,10,256]{4,3,2,1,0:T(8,128)(2,1)S(1)}, bf16[8,1,3,10,256]{4,3,2,1,0:T(8,128)(2,1)S(1)}, u32[]{:S(2)}, u32[]{:S(2)}) collective-permute-start(bf16[8,1,3,10,256]{4,3,2,1,0:T(8,128)(2,1)S(1)} %get-tuple-element.18), channel_id=1, source_target_pairs={{1,0},{2,1},{3,2},{4,3},{5,4},{6,5},{7,6},{9,8},{10,9},{11,10},{12... | collective-permute-start | bytes 368648 | tf_op jit(solution)/shard_map/ppermute | solution.py:31
  (4 other events, 24.9 us)
